TPU v7x, 32 devices: a whole 2x2x4 slice. The times are simulated.
32 devices in a mesh: dp: 4 (over y, x), seq: 2 (over core), tensor: 4 (over z).
Axes of the slice: x: 2, y: 2, z: 4, core: 2. Of those that a mesh axis runs over, the one named last changes fastest.
Arguments:
- block_input: float32 [4, 16, 256, 1024], P('dp', 'seq', 'tensor'), may hold values from -6 to 6
- w_qkv: bfloat16 [1024, 3, 1024], P(None, None, 'tensor'), may hold values from -0.1875 to 0.1875
- qv_bias: bfloat16 [2, 1024], P(None, 'tensor'), may hold values from -3 to 3
- w_out: bfloat16 [1024, 1024], P('tensor'), may hold values from -3 to 3
- b_out: bfloat16 [1024], replicated, may hold values from -3 to 3
- w_up: bfloat16 [1024, 4096], P(None, 'tensor'), may hold values from -0.1875 to 0.1875
- b_up: bfloat16 [4096], P('tensor'), may hold values from -3 to 3
- w_down: bfloat16 [4096, 1024], P('tensor'), may hold values from -0.09375 to 0.09375
- b_down: bfloat16 [1024], replicated, may hold values from -3 to 3
- w_mod: bfloat16 [1024, 6144], replicated, may hold values from -0.375 to 0.375
- b_mod: bfloat16 [6144], replicated, may hold values from -3 to 3
- context_frames: int32 [4], P('dp'), may hold values from 1 to 15
- noise_levels: int32 [4, 16], P('dp', 'seq'), may hold values from 0 to 999
- cotangent: float32 [4, 16, 256, 1024], P('dp', 'seq', 'tensor'), may hold values from -6 to 6
Outputs:
- output: float32 [4, 16, 256, 1024], P('dp', 'seq', 'tensor')
- grad_input: float32 [4, 16, 256, 1024], P('dp', 'seq', 'tensor')
- grad_w_qkv: float32 [1024, 3, 1024], P(None, None, 'tensor')
- grad_qv_bias: float32 [2, 1024], P(None, 'tensor')
- grad_w_out: float32 [1024, 1024], P('tensor')
- grad_b_out: float32 [1024], P('tensor')
- grad_w_up: float32 [1024, 4096], P(None, 'tensor')
- grad_b_up: float32 [4096], P('tensor')
- grad_w_down: float32 [4096, 1024], P('tensor')
- grad_b_down: float32 [1024], P('tensor')
- grad_w_mod: float32 [1024, 6144], P(None, 'tensor')
- grad_b_mod: float32 [6144], P('tensor')
Inputs may be any that keep to these rules, and one draw needn't show every extreme that they name: `noise_levels`: noise level index of each frame.
All inputs are finite; a program needn't handle non-finite values.
Results may differ from a plain program's by a relative error of at most 0.02.
Values may be sent and summed in bfloat16 or wider, within the bound.
No kernel may reach another device: no remote copies, remote signals or barrier semaphores. Data moves between devices by JAX's collectives and lax.ppermute only.
A program may use at most 256 MiB of HBM per device.

v0:
```python
import math
import jax
import jax.numpy as jnp
from jax import lax
from jax.sharding import PartitionSpec as P

HD = 64


def level_features(levels, context, frame_ids, breadth):
    level_used = jnp.where(frame_ids[None, :] < context[:, None], 0, levels).astype(jnp.float32)
    halfway = breadth // 2
    frequency = jnp.exp(-math.log(10000.0) * jnp.arange(halfway, dtype=jnp.float32) / halfway)
    angles = level_used[..., None] * frequency
    return jax.nn.silu(jnp.concatenate([jnp.cos(angles), jnp.sin(angles)], axis=-1))


def normalize(stream):
    centre = stream - jnp.mean(stream, axis=-1, keepdims=True)
    inverse = lax.rsqrt(jnp.mean(centre * centre, axis=-1, keepdims=True) + 1e-06)
    return (centre * inverse, inverse)


def norm_back(grad_normed, normed, inverse):
    first_mean = jnp.mean(grad_normed, axis=-1, keepdims=True)
    second_mean = jnp.mean(grad_normed * normed, axis=-1, keepdims=True)
    return inverse * (grad_normed - first_mean - normed * second_mean)


def gelu_back(pre_act, grad_act):
    _, pullback = jax.vjp(lambda argument: jax.nn.gelu(argument, approximate=True), pre_act)
    return pullback(grad_act)[0]


def body(
    block_input,
    w_qkv,
    qv_bias,
    w_out,
    b_out,
    w_up,
    b_up,
    w_down,
    b_down,
    w_mod,
    b_mod,
    context_frames,
    noise_levels,
    cotangent,
):
    clip_count, half_frames, patch_local, breadth = block_input.shape
    patches_all = patch_local * lax.axis_size("tensor")
    head_cols = w_qkv.shape[2]
    heads_local = head_cols // HD
    softmax_scale = HD ** (-0.5)
    frame_first = lax.axis_index("seq") * half_frames
    frame_ids = frame_first + jnp.arange(half_frames, dtype=jnp.int32)
    condition = level_features(noise_levels, context_frames, frame_ids, breadth).astype(
        jnp.bfloat16
    )
    modulation = jnp.einsum(
        "cfd,de->cfe", condition, w_mod, preferred_element_type=jnp.float32
    ) + b_mod.astype(jnp.float32)
    shift_one, scale_one, gate_one, shift_two, scale_two, gate_two = jnp.split(
        modulation[:, :, None, :], 6, axis=-1
    )
    normed_one, inverse_one = normalize(block_input)
    attn_in = (normed_one * (1.0 + scale_one) + shift_one).astype(jnp.bfloat16)
    attn_all = lax.all_gather(attn_in, "tensor", axis=2, tiled=True)
    projected = jnp.einsum("cfpd,dke->cfpke", attn_all, w_qkv, preferred_element_type=jnp.float32)
    bias_float = qv_bias.astype(jnp.float32)
    queries = (projected[..., 0, :] + bias_float[0]).astype(jnp.bfloat16)
    key_local = projected[..., 1, :].astype(jnp.bfloat16)
    value_local = (projected[..., 2, :] + bias_float[1]).astype(jnp.bfloat16)
    key_clip, value_clip = (
        lax.all_gather(key_local, "seq", axis=1, tiled=True),
        lax.all_gather(value_local, "seq", axis=1, tiled=True),
    )
    query_rows = half_frames * patches_all
    block_rows = min(512, query_rows)
    block_count = query_rows // block_rows
    key_rows = key_clip.shape[1] * patches_all
    key_frame = jnp.arange(key_rows, dtype=jnp.int32) // patches_all
    query_frames = (frame_first + jnp.arange(query_rows, dtype=jnp.int32) // patches_all).reshape(
        block_count, block_rows
    )
    query_heads = queries.reshape(clip_count, block_count, block_rows, heads_local, HD)
    key_heads = key_clip.reshape(clip_count, key_rows, heads_local, HD)
    value_heads = value_clip.reshape(clip_count, key_rows, heads_local, HD)

    def masked_scores(query_block, keys, frames_block, context_limit):
        scores = (
            jnp.einsum("bhd,khd->hbk", query_block, keys, preferred_element_type=jnp.float32)
            * softmax_scale
        )
        allowed = (key_frame[None, :] <= frames_block[:, None]) | (
            key_frame[None, :] < context_limit
        )
        return jnp.where(allowed[None], scores, -1e30)

    def forward_clip(members):
        clip_queries, keys, values, context_limit = members

        def forward_block(slices):
            query_block, frames_block = slices
            scores = masked_scores(query_block, keys, frames_block, context_limit)
            row_max = jnp.max(scores, axis=-1, keepdims=True)
            exponent = jnp.exp(scores - row_max)
            denominator = jnp.sum(exponent, axis=-1, keepdims=True)
            probability = (exponent / denominator).astype(jnp.bfloat16)
            result = jnp.einsum(
                "hbk,khd->bhd", probability, values, preferred_element_type=jnp.float32
            )
            return (result.astype(jnp.bfloat16), (row_max + jnp.log(denominator))[..., 0])

        return lax.map(forward_block, (clip_queries, query_frames))

    attended, log_total = lax.map(
        forward_clip, (query_heads, key_heads, value_heads, context_frames)
    )
    attended_rows = attended.reshape(clip_count, half_frames, patches_all, head_cols)
    portion = attended_rows
    branch_rows = lax.psum_scatter(
        jnp.einsum("cfpe,ed->pcfd", portion, w_out, preferred_element_type=jnp.float32).astype(
            jnp.bfloat16
        ),
        "tensor",
        scatter_dimension=0,
        tiled=True,
    ).astype(jnp.float32)
    branch_one = jnp.transpose(branch_rows, (1, 2, 0, 3)) + b_out.astype(jnp.float32)
    hidden_one = block_input + gate_one * branch_one
    normed_two, inverse_two = normalize(hidden_one)
    mlp_in = (normed_two * (1.0 + scale_two) + shift_two).astype(jnp.bfloat16)
    mlp_all = lax.all_gather(mlp_in, "tensor", axis=2, tiled=True)
    pre_act = jnp.einsum(
        "cfpd,de->cfpe", mlp_all, w_up, preferred_element_type=jnp.float32
    ) + b_up.astype(jnp.float32)
    activated = jax.nn.gelu(pre_act, approximate=True).astype(jnp.bfloat16)
    portion = activated
    mlp_rows = lax.psum_scatter(
        jnp.einsum("cfpe,ed->pcfd", portion, w_down, preferred_element_type=jnp.float32).astype(
            jnp.bfloat16
        ),
        "tensor",
        scatter_dimension=0,
        tiled=True,
    ).astype(jnp.float32)
    mlp_out = jnp.transpose(mlp_rows, (1, 2, 0, 3)) + b_down.astype(jnp.float32)
    output = hidden_one + gate_two * mlp_out
    grad_mlp = gate_two * cotangent
    grad_gate_two = jnp.sum(cotangent * mlp_out, axis=2)
    grad_b_down = jnp.sum(grad_mlp, axis=(0, 1, 2))
    grad_mlp_low = grad_mlp.astype(jnp.bfloat16)
    grad_mlp_all = lax.all_gather(grad_mlp_low, "tensor", axis=2, tiled=True)
    grad_act = jnp.einsum("cfpd,ed->cfpe", grad_mlp_all, w_down, preferred_element_type=jnp.float32)
    grad_w_down = jnp.einsum(
        "cfpe,cfpd->ed", activated, grad_mlp_all, preferred_element_type=jnp.float32
    )
    grad_pre = gelu_back(pre_act, grad_act).astype(jnp.bfloat16)
    grad_b_up = jnp.sum(grad_pre.astype(jnp.float32), axis=(0, 1, 2))
    grad_w_up = jnp.einsum("cfpd,cfpe->de", mlp_all, grad_pre, preferred_element_type=jnp.float32)
    portion = grad_pre
    grad_mlp_rows = lax.psum_scatter(
        jnp.einsum("cfpe,de->pcfd", portion, w_up, preferred_element_type=jnp.float32).astype(
            jnp.bfloat16
        ),
        "tensor",
        scatter_dimension=0,
        tiled=True,
    ).astype(jnp.float32)
    grad_mlp_in = jnp.transpose(grad_mlp_rows, (1, 2, 0, 3))
    grad_shift_two = jnp.sum(grad_mlp_in, axis=2)
    grad_scale_two = jnp.sum(grad_mlp_in * normed_two, axis=2)
    grad_hidden = cotangent + norm_back(grad_mlp_in * (1.0 + scale_two), normed_two, inverse_two)
    grad_branch = gate_one * grad_hidden
    grad_gate_one = jnp.sum(grad_hidden * branch_one, axis=2)
    grad_b_out = jnp.sum(grad_branch, axis=(0, 1, 2))
    grad_branch_all = lax.all_gather(grad_branch.astype(jnp.bfloat16), "tensor", axis=2, tiled=True)
    grad_attended = jnp.einsum(
        "cfpd,ed->cfpe", grad_branch_all, w_out, preferred_element_type=jnp.float32
    ).astype(jnp.bfloat16)
    grad_w_out = jnp.einsum(
        "cfpe,cfpd->ed", attended_rows, grad_branch_all, preferred_element_type=jnp.float32
    )
    grad_heads = grad_attended.reshape(clip_count, block_count, block_rows, heads_local, HD)

    def backward_clip(members):
        clip_queries, keys, values, context_limit, clip_grads, clip_totals = members

        def backward_block(running, slices):
            key_acc, value_acc = running
            query_block, frames_block, grad_block, total_block = slices
            scores = masked_scores(query_block, keys, frames_block, context_limit)
            probability = jnp.exp(scores - total_block[..., None])
            grad_prob = jnp.einsum(
                "bhd,khd->hbk", grad_block, values, preferred_element_type=jnp.float32
            )
            inner_sum = jnp.sum(probability * grad_prob, axis=-1, keepdims=True)
            grad_scores = (probability * (grad_prob - inner_sum)).astype(jnp.bfloat16)
            grad_query = (
                jnp.einsum("hbk,khd->bhd", grad_scores, keys, preferred_element_type=jnp.float32)
                * softmax_scale
            )
            key_acc = (
                key_acc
                + jnp.einsum(
                    "hbk,bhd->khd", grad_scores, query_block, preferred_element_type=jnp.float32
                )
                * softmax_scale
            )
            value_acc = value_acc + jnp.einsum(
                "hbk,bhd->khd",
                probability.astype(jnp.bfloat16),
                grad_block,
                preferred_element_type=jnp.float32,
            )
            return ((key_acc, value_acc), grad_query.astype(jnp.bfloat16))

        empty_acc = jnp.zeros((key_rows, heads_local, HD), jnp.float32)
        (grad_keys, grad_values), grad_queries = lax.scan(
            backward_block,
            (empty_acc, empty_acc),
            (clip_queries, query_frames, clip_grads, clip_totals),
        )
        return (grad_queries, grad_keys, grad_values)

    grad_queries, grad_keys, grad_values = lax.map(
        backward_clip, (query_heads, key_heads, value_heads, context_frames, grad_heads, log_total)
    )
    key_shape = (clip_count, key_clip.shape[1], patches_all, head_cols)
    grad_key_own, grad_value_own = (
        lax.psum_scatter(
            grad_keys.reshape(key_shape).astype(jnp.bfloat16),
            "seq",
            scatter_dimension=1,
            tiled=True,
        ).astype(jnp.float32),
        lax.psum_scatter(
            grad_values.reshape(key_shape).astype(jnp.bfloat16),
            "seq",
            scatter_dimension=1,
            tiled=True,
        ).astype(jnp.float32),
    )
    grad_qkv = jnp.stack(
        [
            grad_queries.reshape(clip_count, half_frames, patches_all, head_cols),
            grad_key_own.astype(jnp.bfloat16),
            grad_value_own.astype(jnp.bfloat16),
        ],
        axis=3,
    )
    grad_w_qkv = jnp.einsum(
        "cfpd,cfpke->dke", attn_all, grad_qkv, preferred_element_type=jnp.float32
    )
    grad_qv_bias = jnp.sum(grad_qkv[:, :, :, 0::2, :].astype(jnp.float32), axis=(0, 1, 2))
    portion = grad_qkv
    grad_attn_rows = lax.psum_scatter(
        jnp.einsum("cfpke,dke->pcfd", portion, w_qkv, preferred_element_type=jnp.float32).astype(
            jnp.bfloat16
        ),
        "tensor",
        scatter_dimension=0,
        tiled=True,
    ).astype(jnp.float32)
    grad_attn_in = jnp.transpose(grad_attn_rows, (1, 2, 0, 3))
    grad_shift_one = jnp.sum(grad_attn_in, axis=2)
    grad_scale_one = jnp.sum(grad_attn_in * normed_one, axis=2)
    grad_input = grad_hidden + norm_back(grad_attn_in * (1.0 + scale_one), normed_one, inverse_one)
    grad_modulation = jnp.concatenate(
        [
            grad_shift_one,
            grad_scale_one,
            grad_gate_one,
            grad_shift_two,
            grad_scale_two,
            grad_gate_two,
        ],
        axis=-1,
    )
    grad_modulation = grad_modulation.reshape(clip_count * half_frames, 6 * breadth)
    modulation_cols, out_bias_part, down_bias_part = (
        lax.psum_scatter(
            grad_modulation.astype(jnp.bfloat16), "tensor", scatter_dimension=1, tiled=True
        ).astype(jnp.float32),
        lax.psum_scatter(
            grad_b_out.astype(jnp.bfloat16), "tensor", scatter_dimension=0, tiled=True
        ).astype(jnp.float32),
        lax.psum_scatter(
            grad_b_down.astype(jnp.bfloat16), "tensor", scatter_dimension=0, tiled=True
        ).astype(jnp.float32),
    )
    condition_rows = condition.reshape(clip_count * half_frames, breadth).astype(jnp.float32)
    grad_w_mod = jnp.dot(condition_rows.T, modulation_cols, precision=lax.Precision.HIGHEST)
    grad_b_mod = jnp.sum(modulation_cols, axis=0)
    (
        total_w_qkv,
        total_qv_bias,
        total_w_out,
        total_b_out,
        total_w_up,
        total_b_up,
        total_w_down,
        total_b_down,
        total_w_mod,
        total_b_mod,
    ) = (
        lax.psum(grad_w_qkv.astype(jnp.bfloat16), ("dp", "seq")).astype(jnp.float32),
        lax.psum(grad_qv_bias.astype(jnp.bfloat16), ("dp", "seq")).astype(jnp.float32),
        lax.psum(grad_w_out.astype(jnp.bfloat16), ("dp", "seq")).astype(jnp.float32),
        lax.psum(out_bias_part.astype(jnp.bfloat16), ("dp", "seq")).astype(jnp.float32),
        lax.psum(grad_w_up.astype(jnp.bfloat16), ("dp", "seq")).astype(jnp.float32),
        lax.psum(grad_b_up.astype(jnp.bfloat16), ("dp", "seq")).astype(jnp.float32),
        lax.psum(grad_w_down.astype(jnp.bfloat16), ("dp", "seq")).astype(jnp.float32),
        lax.psum(down_bias_part.astype(jnp.bfloat16), ("dp", "seq")).astype(jnp.float32),
        lax.psum(grad_w_mod.astype(jnp.bfloat16), ("dp", "seq")).astype(jnp.float32),
        lax.psum(grad_b_mod.astype(jnp.bfloat16), ("dp", "seq")).astype(jnp.float32),
    )
    return (
        output,
        grad_input,
        total_w_qkv,
        total_qv_bias,
        total_w_out,
        total_b_out,
        total_w_up,
        total_b_up,
        total_w_down,
        total_b_down,
        total_w_mod,
        total_b_mod,
    )


def solution(mesh):
    placed = (
        P("dp", "seq", "tensor", None),
        P(None, None, "tensor"),
        P(None, "tensor"),
        P("tensor", None),
        P(),
        P(None, "tensor"),
        P("tensor"),
        P("tensor", None),
        P(),
        P(),
        P(),
        P("dp"),
        P("dp", "seq"),
        P("dp", "seq", "tensor", None),
    )
    return jax.shard_map(
        body,
        mesh=mesh,
        in_specs=placed,
        out_specs=(
            P("dp", "seq", "tensor", None),
            P("dp", "seq", "tensor", None),
            P(None, None, "tensor"),
            P(None, "tensor"),
            P("tensor", None),
            P("tensor"),
            P(None, "tensor"),
            P("tensor"),
            P("tensor", None),
            P("tensor"),
            P(None, "tensor"),
            P("tensor"),
        ),
        check_vma=False,
    )
```

profile of v0, /device:TPU:0, one launch (start us, length us, event | category | flops | bytes accessed | tf_op | source)
XLA Modules:
  0.0 1632.9 jit_solution(15091767421687436867)
XLA Ops:
  12.0 6.5 fusion.60
  21.3 83.5 %all-gather.8.cloned.1.call-done = bf16[1,8,256,1024]{3,2,1,0:T(8,128)(2,1)} async-done(((bf16[1,8,64,1024]{3,2,1,0:T(8,128)(2,1)}), bf16[1,8,256,1024]{3,2,1,0:T(8,128)(2,1)}) %all-gather.8.cloned.1.call-update) | async-done | bytes 4194320 | tf_op jit(solution)/shard_map/all_gather | solution.py:69
  104.9 5.7 fusion.79
  130.0 4.5 copy.82
  138.8 4.5 copy.80
  147.6 198.6 %while.50 = (s32[]{:T(128)}, bf16[4,512,4,64]{1,3,2,0:T(8,128)(2,1)S(1)}, f32[4,4,512]{2,1,0:T(4,128)S(1)}, s32[4,512]{1,0:T(4,128)S(1)}, s32[]{:T(128)}, /*inde...) while((s32[]{:T(128)}, ...), condition=%wide.region_5.6_spmd.clone.clone, body=%wide.region_2.5_spmd.clone.clone.sunk | while | flops 2252539904 | bytes 122271888 | solution.py:116
  150.0 16.0 fusion.176
  166.1 15.0 fusion.177
  181.1 16.3 fusion.178
  199.6 16.0 fusion.176
  215.7 15.0 fusion.177
  230.7 16.3 fusion.178
  249.2 16.0 fusion.176
  265.3 15.0 fusion.177
  280.3 16.3 fusion.178
  298.8 16.0 fusion.176
  314.9 15.0 fusion.177
  329.9 16.3 fusion.178
  349.8 4.8 convert_bitcast_fusion.2
  354.7 76.7 %reduce-scatter.8.cloned.1.call-done = bf16[64,1,8,1024]{3,0,2,1:T(8,128)(2,1)} async-done(((bf16[256,1,8,1024]{3,0,2,1:T(8,128)(2,1)}), bf16[64,1,8,1024]{3,0,2,1:T(8,128)(2,1)}) %reduce-scatter.8.cloned.1.call-update) | async-done | bytes 1048592 | tf_op jit(solution)/shard_map/reduce_scatter | solution.py:123
  436.6 81.3 %all-gather.12.cloned.1.call-done = bf16[1,8,256,1024]{3,2,1,0:T(8,128)(2,1)} async-done(((bf16[1,8,64,1024]{3,2,1,0:T(8,128)(2,1)}), bf16[1,8,256,1024]{3,2,1,0:T(8,128)(2,1)}) %all-gather.12.cloned.1.call-update) | async-done | bytes 4194320 | tf_op jit(solution)/shard_map/all_gather | solution.py:135
  517.9 6.9 fusion.75
  528.1 7.0 convert_bitcast_fusion.1
  535.7 74.8 %reduce-scatter.10.cloned.1.call-done = bf16[64,1,8,1024]{3,0,2,1:T(8,128)(2,1)} async-done(((bf16[256,1,8,1024]{3,0,2,1:T(8,128)(2,1)}), bf16[64,1,8,1024]{3,0,2,1:T(8,128)(2,1)}) %reduce-scatter.10.cloned.1.call-update) | async-done | bytes 1048592 | tf_op jit(solution)/shard_map/reduce_scatter | solution.py:141
  614.5 81.4 %all-gather.14.cloned.1.call-done = bf16[1,8,256,1024]{3,2,1,0:T(8,128)(2,1)} async-done(((bf16[1,8,64,1024]{3,2,1,0:T(8,128)(2,1)}), bf16[1,8,256,1024]{3,2,1,0:T(8,128)(2,1)}) %all-gather.14.cloned.1.call-update) | async-done | bytes 4194320 | tf_op jit(solution)/shard_map/all_gather | solution.py:155
  695.9 13.3 fusion.144
  711.2 6.2 convert_bitcast_fusion
  717.5 75.4 %reduce-scatter.12.cloned.1.call-done = bf16[64,1,8,1024]{3,0,2,1:T(8,128)(2,1)} async-done(((bf16[256,1,8,1024]{3,0,2,1:T(8,128)(2,1)}), bf16[64,1,8,1024]{3,0,2,1:T(8,128)(2,1)}) %reduce-scatter.12.cloned.1.call-update) | async-done | bytes 1048592 | tf_op jit(solution)/shard_map/reduce_scatter | solution.py:164
  803.0 81.3 %all-gather.16.cloned.1.call-done = bf16[1,8,256,1024]{3,2,1,0:T(8,128)(2,1)} async-done(((bf16[1,8,64,1024]{3,2,1,0:T(8,128)(2,1)}), bf16[1,8,256,1024]{3,2,1,0:T(8,128)(2,1)}) %all-gather.16.cloned.1.call-update) | async-done | bytes 4194320 | tf_op jit(solution)/shard_map/all_gather | solution.py:179
  892.2 435.7 %while.51 = (s32[]{:T(128)}, f32[4096,4,64]{0,2,1:T(8,128)}, f32[4096,4,64]{0,2,1:T(8,128)}, bf16[4,512,4,64]{1,3,2,0:T(8,128)(2,1)}, bf16[4,512,4,64]{1,3,2,0:T...) while((s32[]{:T(128)}, f32[4096,4,64]{0,2,1:T(8,128)}, ...), condition=%wide.region_15.16_spmd.clone.clone, body=%wide.region_13.15_spmd.clone.clone.sunk | while | flops 5504305152 | bytes 351639744 | solution.py:221
  894.6 17.3 %fusion.188 = f32[4,512,4096]{2,1,0:T(8,128)} fusion(bf16[4096,4,64]{0,2,1:T(8,128)(2,1)} %get-tuple-element.645, bf16[4,512,4,64]{1,3,2,0:T(8,128)(2,1)} %get-tuple-element.642, s32[]{:T(128)S(6)} %copy.131), kind=kOutput, calls=%fused_computation.48.clone.1 | convolution fusion | flops 1073741824 | bytes 35913732 | tf_op jit(solution)/shard_map/while/body/eval_jaxpr/while/body/eval_jaxpr/bhd,khd->hbk/dot_general | solution.py:93
  911.9 16.5 %fusion.190 = f32[4096,4,64]{0,2,1:T(8,128)} fusion(f32[4,512,4096]{2,1,0:T(8,128)} %fusion.188, f32[4,512]{1,0:T(4,128)S(1)} %dynamic-slice_bitcast_fusion.2, pred[512,4096]{1,0:T(8,128)(4,1)S(1)} %compare_or_fusion.5, f32[4096,4,64]{0,2,1:T(8,128)} %get-tuple-element.627, pred[]{:T(512)S(6)} %compare.9, ...), kind=kOutput, calls=%fused_computation.39.clone.1 | convolution fusion | flops 1109393408 | bytes 44310532 | tf_op jit(solution)/shard_map/while/body/eval_jaxpr/while/body/eval_jaxpr/hbk,bhd->khd/dot_general | solution.py:212
  928.4 25.9 %multiply_reduce_fusion.6 = (f32[4,512]{1,0:T(4,128)S(1)}, f32[4,512,4096]{2,1,0:T(8,128)}) fusion(f32[4,512,4096]{2,1,0:T(8,128)} %fusion.188, f32[4,512]{1,0:T(4,128)S(1)} %dynamic-slice_bitcast_fusion.2, pred[512,4096]{1,0:T(8,128)(4,1)S(1)} %compare_or_fusion.5, bf16[4096,4,64]{0,2,1:T(8,128)(2,1)} %get-tuple-element.648, ...), kind=kOutput, calls=%fused_computation.29.clone.1 | convolution fusion | flops 1115682816 | bytes 71581696 | tf_op jit(solution)/shard_map/while/body/eval_jaxpr/while/body/eval_jaxpr/bhd,khd->hbk/dot_general | solution.py:196
  954.3 27.6 %multiply_convert_fusion.10 = bf16[4,512,4096]{2,1,0:T(8,128)(2,1)} fusion(f32[4,512,4096]{2,1,0:T(8,128)} %get-tuple-element.583, f32[4,512,4096]{2,1,0:T(8,128)} %fusion.188, f32[4,512]{1,0:T(4,128)S(1)} %get-tuple-element.584, f32[4,512]{1,0:T(4,128)S(1)} %dynamic-slice_bitcast_fusion.2, pred[512,4096]{1,0:T(8,128)(4,1)S(1)} %compare_or_fusion.5), kind=kLoop, calls=%fused_computation.28.clone.1 | loop fusion | flops 50331648 | bytes 85999616 | tf_op jit(solution)/shard_map/while/body/eval_jaxpr/while/body/eval_jaxpr/convert_element_type | solution.py:200
  981.9 10.1 fusion.191
  993.2 6.1 fusion.189
  1001.5 17.3 %fusion.188 = f32[4,512,4096]{2,1,0:T(8,128)} fusion(bf16[4096,4,64]{0,2,1:T(8,128)(2,1)} %get-tuple-element.645, bf16[4,512,4,64]{1,3,2,0:T(8,128)(2,1)} %get-tuple-element.642, s32[]{:T(128)S(6)} %copy.131), kind=kOutput, calls=%fused_computation.48.clone.1 | convolution fusion | flops 1073741824 | bytes 35913732 | tf_op jit(solution)/shard_map/while/body/eval_jaxpr/while/body/eval_jaxpr/bhd,khd->hbk/dot_general | solution.py:93
  1018.8 17.7 %fusion.190 = f32[4096,4,64]{0,2,1:T(8,128)} fusion(f32[4,512,4096]{2,1,0:T(8,128)} %fusion.188, f32[4,512]{1,0:T(4,128)S(1)} %dynamic-slice_bitcast_fusion.2, pred[512,4096]{1,0:T(8,128)(4,1)S(1)} %compare_or_fusion.5, f32[4096,4,64]{0,2,1:T(8,128)} %get-tuple-element.627, pred[]{:T(512)S(6)} %compare.9, ...), kind=kOutput, calls=%fused_computation.39.clone.1 | convolution fusion | flops 1109393408 | bytes 44310532 | tf_op jit(solution)/shard_map/while/body/eval_jaxpr/while/body/eval_jaxpr/hbk,bhd->khd/dot_general | solution.py:212
  1036.5 25.9 %multiply_reduce_fusion.6 = (f32[4,512]{1,0:T(4,128)S(1)}, f32[4,512,4096]{2,1,0:T(8,128)}) fusion(f32[4,512,4096]{2,1,0:T(8,128)} %fusion.188, f32[4,512]{1,0:T(4,128)S(1)} %dynamic-slice_bitcast_fusion.2, pred[512,4096]{1,0:T(8,128)(4,1)S(1)} %compare_or_fusion.5, bf16[4096,4,64]{0,2,1:T(8,128)(2,1)} %get-tuple-element.648, ...), kind=kOutput, calls=%fused_computation.29.clone.1 | convolution fusion | flops 1115682816 | bytes 71581696 | tf_op jit(solution)/shard_map/while/body/eval_jaxpr/while/body/eval_jaxpr/bhd,khd->hbk/dot_general | solution.py:196
  1062.4 27.6 %multiply_convert_fusion.10 = bf16[4,512,4096]{2,1,0:T(8,128)(2,1)} fusion(f32[4,512,4096]{2,1,0:T(8,128)} %get-tuple-element.583, f32[4,512,4096]{2,1,0:T(8,128)} %fusion.188, f32[4,512]{1,0:T(4,128)S(1)} %get-tuple-element.584, f32[4,512]{1,0:T(4,128)S(1)} %dynamic-slice_bitcast_fusion.2, pred[512,4096]{1,0:T(8,128)(4,1)S(1)} %compare_or_fusion.5), kind=kLoop, calls=%fused_computation.28.clone.1 | loop fusion | flops 50331648 | bytes 85999616 | tf_op jit(solution)/shard_map/while/body/eval_jaxpr/while/body/eval_jaxpr/convert_element_type | solution.py:200
  1090.0 10.1 fusion.191
  1101.2 7.4 fusion.189
  1110.9 17.3 %fusion.188 = f32[4,512,4096]{2,1,0:T(8,128)} fusion(bf16[4096,4,64]{0,2,1:T(8,128)(2,1)} %get-tuple-element.645, bf16[4,512,4,64]{1,3,2,0:T(8,128)(2,1)} %get-tuple-element.642, s32[]{:T(128)S(6)} %copy.131), kind=kOutput, calls=%fused_computation.48.clone.1 | convolution fusion | flops 1073741824 | bytes 35913732 | tf_op jit(solution)/shard_map/while/body/eval_jaxpr/while/body/eval_jaxpr/bhd,khd->hbk/dot_general | solution.py:93
  1128.2 17.7 %fusion.190 = f32[4096,4,64]{0,2,1:T(8,128)} fusion(f32[4,512,4096]{2,1,0:T(8,128)} %fusion.188, f32[4,512]{1,0:T(4,128)S(1)} %dynamic-slice_bitcast_fusion.2, pred[512,4096]{1,0:T(8,128)(4,1)S(1)} %compare_or_fusion.5, f32[4096,4,64]{0,2,1:T(8,128)} %get-tuple-element.627, pred[]{:T(512)S(6)} %compare.9, ...), kind=kOutput, calls=%fused_computation.39.clone.1 | convolution fusion | flops 1109393408 | bytes 44310532 | tf_op jit(solution)/shard_map/while/body/eval_jaxpr/while/body/eval_jaxpr/hbk,bhd->khd/dot_general | solution.py:212
  1145.9 25.9 %multiply_reduce_fusion.6 = (f32[4,512]{1,0:T(4,128)S(1)}, f32[4,512,4096]{2,1,0:T(8,128)}) fusion(f32[4,512,4096]{2,1,0:T(8,128)} %fusion.188, f32[4,512]{1,0:T(4,128)S(1)} %dynamic-slice_bitcast_fusion.2, pred[512,4096]{1,0:T(8,128)(4,1)S(1)} %compare_or_fusion.5, bf16[4096,4,64]{0,2,1:T(8,128)(2,1)} %get-tuple-element.648, ...), kind=kOutput, calls=%fused_computation.29.clone.1 | convolution fusion | flops 1115682816 | bytes 71581696 | tf_op jit(solution)/shard_map/while/body/eval_jaxpr/while/body/eval_jaxpr/bhd,khd->hbk/dot_general | solution.py:196
  1171.8 27.6 %multiply_convert_fusion.10 = bf16[4,512,4096]{2,1,0:T(8,128)(2,1)} fusion(f32[4,512,4096]{2,1,0:T(8,128)} %get-tuple-element.583, f32[4,512,4096]{2,1,0:T(8,128)} %fusion.188, f32[4,512]{1,0:T(4,128)S(1)} %get-tuple-element.584, f32[4,512]{1,0:T(4,128)S(1)} %dynamic-slice_bitcast_fusion.2, pred[512,4096]{1,0:T(8,128)(4,1)S(1)} %compare_or_fusion.5), kind=kLoop, calls=%fused_computation.28.clone.1 | loop fusion | flops 50331648 | bytes 85999616 | tf_op jit(solution)/shard_map/while/body/eval_jaxpr/while/body/eval_jaxpr/convert_element_type | solution.py:200
  1199.4 10.1 fusion.191
  1210.7 7.4 fusion.189
  1220.3 17.3 %fusion.188 = f32[4,512,4096]{2,1,0:T(8,128)} fusion(bf16[4096,4,64]{0,2,1:T(8,128)(2,1)} %get-tuple-element.645, bf16[4,512,4,64]{1,3,2,0:T(8,128)(2,1)} %get-tuple-element.642, s32[]{:T(128)S(6)} %copy.131), kind=kOutput, calls=%fused_computation.48.clone.1 | convolution fusion | flops 1073741824 | bytes 35913732 | tf_op jit(solution)/shard_map/while/body/eval_jaxpr/while/body/eval_jaxpr/bhd,khd->hbk/dot_general | solution.py:93
  1237.6 17.7 %fusion.190 = f32[4096,4,64]{0,2,1:T(8,128)} fusion(f32[4,512,4096]{2,1,0:T(8,128)} %fusion.188, f32[4,512]{1,0:T(4,128)S(1)} %dynamic-slice_bitcast_fusion.2, pred[512,4096]{1,0:T(8,128)(4,1)S(1)} %compare_or_fusion.5, f32[4096,4,64]{0,2,1:T(8,128)} %get-tuple-element.627, pred[]{:T(512)S(6)} %compare.9, ...), kind=kOutput, calls=%fused_computation.39.clone.1 | convolution fusion | flops 1109393408 | bytes 44310532 | tf_op jit(solution)/shard_map/while/body/eval_jaxpr/while/body/eval_jaxpr/hbk,bhd->khd/dot_general | solution.py:212
  1255.3 25.9 %multiply_reduce_fusion.6 = (f32[4,512]{1,0:T(4,128)S(1)}, f32[4,512,4096]{2,1,0:T(8,128)}) fusion(f32[4,512,4096]{2,1,0:T(8,128)} %fusion.188, f32[4,512]{1,0:T(4,128)S(1)} %dynamic-slice_bitcast_fusion.2, pred[512,4096]{1,0:T(8,128)(4,1)S(1)} %compare_or_fusion.5, bf16[4096,4,64]{0,2,1:T(8,128)(2,1)} %get-tuple-element.648, ...), kind=kOutput, calls=%fused_computation.29.clone.1 | convolution fusion | flops 1115682816 | bytes 71581696 | tf_op jit(solution)/shard_map/while/body/eval_jaxpr/while/body/eval_jaxpr/bhd,khd->hbk/dot_general | solution.py:196
  1281.2 27.6 %multiply_convert_fusion.10 = bf16[4,512,4096]{2,1,0:T(8,128)(2,1)} fusion(f32[4,512,4096]{2,1,0:T(8,128)} %get-tuple-element.583, f32[4,512,4096]{2,1,0:T(8,128)} %fusion.188, f32[4,512]{1,0:T(4,128)S(1)} %get-tuple-element.584, f32[4,512]{1,0:T(4,128)S(1)} %dynamic-slice_bitcast_fusion.2, pred[512,4096]{1,0:T(8,128)(4,1)S(1)} %compare_or_fusion.5), kind=kLoop, calls=%fused_computation.28.clone.1 | loop fusion | flops 50331648 | bytes 85999616 | tf_op jit(solution)/shard_map/while/body/eval_jaxpr/while/body/eval_jaxpr/convert_element_type | solution.py:200
  1308.8 10.1 fusion.191
  1320.1 7.4 fusion.189
  1348.5 10.5 reduce-scatter.16.cloned.1.call-done
  1359.0 7.5 fusion.61
  1366.8 9.5 bitcast_convert_fusion.2
  1376.3 11.0 bitcast_convert_fusion.1
  1389.7 55.0 %reduce-scatter.18.cloned.1.call-done = bf16[64,1,8,1024]{3,0,2,1:T(8,128)(2,1)} async-done(((bf16[256,1,8,1024]{3,0,2,1:T(8,128)(2,1)}), bf16[64,1,8,1024]{3,0,2,1:T(8,128)(2,1)}) %reduce-scatter.18.cloned.1.call-update) | async-done | bytes 1048592 | tf_op jit(solution)/shard_map/reduce_scatter | solution.py:259
  1449.5 7.5 bitcast_convert_fusion.3
  1457.0 12.5 reduce-scatter.20.cloned.1.call-done
  1474.8 8.9 all-reduce.4
  1488.5 13.2 all-reduce.2
  1504.7 106.7 %all-reduce.7.cloned.1.call-done = (bf16[1024,3,256]{2,0,1:T(8,128)(2,1)}, bf16[256,1024]{1,0:T(8,128)(2,1)}, bf16[1024,1024]{1,0:T(8,128)(2,1)}, bf16[1024,1024]{1,0:T(8,128)(2,1)}, bf16[1024,1536]{1,0:T(8,128)(2,1)}) async-done(((bf16[1024,3,256]{2,0,1:T(8,128)(2,1)}, bf16[256,1024]{1,0:T(8,128)(2,1)}, bf16[1024,1024]{1,0:T(8,128)(2,1)}, bf16[1024,1024]{1,0:T(8,128)(2,1)}, bf16[1024,1536]{1,0:T(8,128)(2,1)}), ...) | async-done | bytes 9437200 | tf_op jit(solution)/shard_map/psum | solution.py:309
  (284 shorter events, 147.7 us)
Async XLA Ops:
  7.2 520.9 %copy-start = (bf16[1024,1024]{1,0:T(8,128)(2,1)S(1)}, bf16[1024,1024]{1,0:T(8,128)(2,1)}, u32[]{:S(2)}) copy-start(bf16[1024,1024]{1,0:T(8,128)(2,1)} %param.25) | copy-start | bytes 6291460
  7.2 4.6 copy-start.41
  7.2 4.6 copy-start.51
  7.2 97.7 %all-gather.8.cloned.1.call-start = ((), (), s32[]{:S(2)}) async-start(), calls=%async_computation.7 | async-start | bytes 5242880 | tf_op jit(solution)/shard_map/all_gather | solution.py:69
  9.8 9.3 copy-start.33
  11.8 7.4 copy-start.36
  12.0 6.5 copy-start.27
  12.0 6.5 copy-start.29
  12.0 7.7 copy-start.4
  18.5 2.8 copy-start.44
  21.3 108.8 %all-gather.10.cloned.1.call-start = ((), (), s32[]{:S(2)}) async-start(), calls=%async_computation.8 | async-start | bytes 3145728 | tf_op jit(solution)/shard_map/all_gather | solution.py:77
  110.5 2.7 copy-start.13
  114.4 24.4 %all-gather.18.cloned.1.call-start = ((), (), s32[]{:S(2)}) async-start(), calls=%async_computation.19 | async-start | bytes 3145728 | tf_op jit(solution)/shard_map/all_gather | solution.py:76
  117.2 314.2 %reduce-scatter.8.cloned.1.call-start = ((), (), s32[]{:S(2)}) async-start(), calls=%async_computation.9 | async-start | bytes 5242880 | tf_op jit(solution)/shard_map/reduce_scatter | solution.py:123
  150.0 16.0 copy-start.3
  199.6 16.0 copy-start.3
  249.2 16.0 copy-start.3
  298.8 16.0 copy-start.3
  349.8 4.8 copy-start.15
  349.8 4.9 copy-start.47
  349.8 81.6 %copy-start.23 = (f32[8,1024]{1,0:T(8,128)S(1)}, f32[8,1024]{1,0:T(8,128)}, u32[]{:S(2)}) copy-start(f32[8,1024]{1,0:T(8,128)} %get-tuple-element.454) | copy-start | bytes 98308
  354.6 80.4 %copy-start.24 = (f32[8,1024]{1,0:T(8,128)S(1)}, f32[8,1024]{1,0:T(8,128)}, u32[]{:S(2)}) copy-start(f32[8,1024]{1,0:T(8,128)} %get-tuple-element.451) | copy-start | bytes 98308
  354.6 80.4 %copy-start.32 = (f32[8,1024]{1,0:T(8,128)S(1)}, f32[8,1024]{1,0:T(8,128)}, u32[]{:S(2)}) copy-start(f32[8,1024]{1,0:T(8,128)} %get-tuple-element.450) | copy-start | bytes 98308
  354.6 163.3 %all-gather.12.cloned.1.call-start = ((), (), s32[]{:S(2)}) async-start(), calls=%async_computation.10 | async-start | bytes 5242880 | tf_op jit(solution)/shard_map/all_gather | solution.py:135
  433.7 2.8 copy-start.48
  436.5 174.0 %reduce-scatter.10.cloned.1.call-start = ((), (), s32[]{:S(2)}) async-start(), calls=%async_computation.11 | async-start | bytes 5242880 | tf_op jit(solution)/shard_map/reduce_scatter | solution.py:141
  436.6 259.3 %copy-start.45 = (f32[1024]{0:T(1024)}, f32[1024]{0:T(1024)S(1)}, u32[]{:S(2)}) copy-start(f32[1024]{0:T(1024)S(1)} %convert_element_type.268) | copy-start | bytes 12292
  524.9 3.2 copy-start.57
  535.0 75.5 %copy-start.26 = (f32[8,1024]{1,0:T(8,128)S(1)}, f32[8,1024]{1,0:T(8,128)}, u32[]{:S(2)}) copy-start(f32[8,1024]{1,0:T(8,128)} %get-tuple-element.449) | copy-start | bytes 98308
  535.1 160.8 %all-gather.14.cloned.1.call-start = ((), (), s32[]{:S(2)}) async-start(), calls=%async_computation.12 | async-start | bytes 5242880 | tf_op jit(solution)/shard_map/all_gather | solution.py:155
  614.4 178.5 %reduce-scatter.12.cloned.1.call-start = ((), (), s32[]{:S(2)}) async-start(), calls=%async_computation.13 | async-start | bytes 5242880 | tf_op jit(solution)/shard_map/reduce_scatter | solution.py:164
  695.8 15.4 copy-start.54
  717.4 75.5 %copy-start.7 = (f32[1,8,64,1024]{3,2,1,0:T(8,128)S(1)}, f32[1,8,64,1024]{3,2,1,0:T(8,128)}, u32[]{:S(2)}) copy-start(f32[1,8,64,1024]{3,2,1,0:T(8,128)} %copy-done.6) | copy-start | bytes 6291460
  717.4 78.4 %copy-start.17 = (bf16[64,1,8,1024]{3,0,2,1:T(8,128)(2,1)S(1)}, bf16[64,1,8,1024]{3,0,2,1:T(8,128)(2,1)}, u32[]{:S(2)}) copy-start(bf16[64,1,8,1024]{3,0,2,1:T(8,128)(2,1)} %reduce-scatter.8.cloned.1.call-done) | copy-start | bytes 3145732
  717.5 166.9 %all-gather.16.cloned.1.call-start = ((), (), s32[]{:S(2)}) async-start(), calls=%async_computation.14 | async-start | bytes 5242880 | tf_op jit(solution)/shard_map/all_gather | solution.py:179
  792.9 3.0 copy-start.12
  800.4 84.0 %copy-start.25 = (bf16[256,1024]{1,0:T(8,128)(2,1)S(1)}, bf16[256,1024]{1,0:T(8,128)(2,1)}, u32[]{:S(2)}) copy-start(bf16[256,1024]{1,0:T(8,128)(2,1)} %param.21) | copy-start | bytes 1572868
  803.0 545.5 %reduce-scatter.14.cloned.1.call-start = ((), (), s32[]{:S(2)}) async-start(), calls=%async_computation.15 | async-start | bytes 3145728 | tf_op jit(solution)/shard_map/reduce_scatter | solution.py:233
  981.9 11.2 copy-start.2
  1090.0 11.2 copy-start.2
  1199.4 11.2 copy-start.2
  1308.8 11.2 copy-start.2
  1336.7 22.3 %reduce-scatter.16.cloned.1.call-start = ((), (), s32[]{:S(2)}) async-start(), calls=%async_computation.16 | async-start | bytes 3145728 | tf_op jit(solution)/shard_map/reduce_scatter | solution.py:239
  1341.2 4.5 copy-start.14
  1345.6 99.1 %reduce-scatter.18.cloned.1.call-start = ((), (), s32[]{:S(2)}) async-start(), calls=%async_computation.17 | async-start | bytes 5242880 | tf_op jit(solution)/shard_map/reduce_scatter | solution.py:259
  1366.6 9.7 copy-start.46
  1366.6 102.9 %reduce-scatter.20.cloned.1.call-start = ((), (), s32[]{:S(2)}) async-start(), calls=%async_computation.18 | async-start | bytes 122880 | tf_op jit(solution)/shard_map/reduce_scatter | solution.py:284
  1366.8 9.5 copy-start.52
  1376.3 11.1 copy-start.11
  1376.3 11.3 copy-start.16
  1376.3 11.3 copy-start.53
  1387.6 58.6 %copy-start.5 = (f32[1,8,64,1024]{3,2,1,0:T(8,128)S(1)}, f32[1,8,64,1024]{3,2,1,0:T(8,128)}, u32[]{:S(2)}) copy-start(f32[1,8,64,1024]{3,2,1,0:T(8,128)} %param.18) | copy-start | bytes 6291460
  1387.6 58.6 %copy-start.22 = (f32[8,1024]{1,0:T(8,128)S(1)}, f32[8,1024]{1,0:T(8,128)}, u32[]{:S(2)}) copy-start(f32[8,1024]{1,0:T(8,128)} %copy-done.21) | copy-start | bytes 98308
  1387.6 58.6 %copy-start.34 = (f32[8,64]{1,0:T(8,128)S(1)}, f32[8,64]{1,0:T(8,128)}, u32[]{:S(2)}) copy-start(f32[8,64]{1,0:T(8,128)} %copy-done.33) | copy-start | bytes 6148
  1387.6 58.6 %copy-start.37 = (f32[8,64]{1,0:T(8,128)S(1)}, f32[8,64]{1,0:T(8,128)}, u32[]{:S(2)}) copy-start(f32[8,64]{1,0:T(8,128)} %copy-done.36) | copy-start | bytes 6148
  1389.7 59.0 %copy-start.40 = (bf16[8,1024]{1,0:T(8,128)(2,1)S(1)}, bf16[8,1024]{1,0:T(8,128)(2,1)}, u32[]{:S(2)}) copy-start(bf16[8,1024]{1,0:T(8,128)(2,1)} %get-tuple-element.386) | copy-start | bytes 49156
  1389.7 59.0 %copy-start.39 = (bf16[8,1024]{1,0:T(8,128)(2,1)S(1)}, bf16[8,1024]{1,0:T(8,128)(2,1)}, u32[]{:S(2)}) copy-start(bf16[8,1024]{1,0:T(8,128)(2,1)} %get-tuple-element.380) | copy-start | bytes 49156
  1389.7 59.0 %copy-start.38 = (bf16[8,1024]{1,0:T(8,128)(2,1)S(1)}, bf16[8,1024]{1,0:T(8,128)(2,1)}, u32[]{:S(2)}) copy-start(bf16[8,1024]{1,0:T(8,128)(2,1)} %get-tuple-element.384) | copy-start | bytes 49156
  1449.4 20.0 %copy-start.28 = (f32[8,512]{1,0:T(8,128)S(1)}, f32[8,512]{1,0:T(8,128)}, u32[]{:S(2)}) copy-start(f32[8,512]{1,0:T(8,128)} %copy-done.27) | copy-start | bytes 49156
  1449.5 20.0 %copy-start.30 = (f32[8,512]{1,0:T(8,128)S(1)}, f32[8,512]{1,0:T(8,128)}, u32[]{:S(2)}) copy-start(f32[8,512]{1,0:T(8,128)} %copy-done.29) | copy-start | bytes 49156
  1449.5 161.9 %all-reduce.7.cloned.1.call-start = ((), (), s32[]{:S(2)}) async-start(), calls=%async_computation.20 | async-start | bytes 18874368 | tf_op jit(solution)/shard_map/psum | solution.py:309
  1611.4 5.6 copy-start.20
  1619.5 3.0 copy-start.18
  1622.0 4.1 copy-start.1
  (14 other events, 23.1 us)
Sparse Core Ops, SparseCore 0:
  21.4 83.4 all-gather.7
  114.6 9.0 all-gather.9
  125.8 11.7 all-gather.17
  354.7 76.6 reduce-scatter.7
  436.6 81.2 all-gather.11
  535.2 75.2 reduce-scatter.9
  614.6 81.2 all-gather.13
  717.6 75.2 reduce-scatter.11
  803.1 81.2 all-gather.15
  1336.8 8.2 reduce-scatter.13
  1347.9 11.0 reduce-scatter.15
  1366.7 78.0 reduce-scatter.17
  1449.6 19.8 reduce-scatter.19
  1474.8 136.5 all-reduce.6
where the time goes:
time: 1640 us; the launch traced here: 1630 us
  waiting for transfers between devices  739 us (45%)
  matrix products  536 us (33%)
  other arithmetic  244 us (15%)
  local copies, waits for them, and re-layouts  73.1 us (4%)
  blocking collectives  22.1 us (1%)
  between operations  16.4 us (1%)
    dot_general x8, matrix products, masked_scores(): jnp.einsum('bhd,khd->hbk', query_block, keys, preferred_element_type=jnp....  133 us
    convert_element_type x4, other arithmetic, backward_block(): grad_scores = (probability * (grad_prob - inner_sum)).astype(jnp.bfloat16)  110 us
    psum x1, waiting for transfers between devices, body(): lax.psum(grad_w_qkv.astype(jnp.bfloat16), ('dp', 'seq')).astype(jnp.float32)  107 us
    dot_general x4, matrix products, backward_block(): jnp.einsum('bhd,khd->hbk', grad_block, values, preferred_element_type=jnp...  104 us
    all_gather x1, waiting for transfers between devices, body(): attn_all = lax.all_gather(attn_in, 'tensor', axis=2, tiled=True)  83.5 us
    all_gather x1, waiting for transfers between devices, body(): grad_mlp_all = lax.all_gather(grad_mlp_low, 'tensor', axis=2, tiled=True)  81.4 us
    all_gather x1, waiting for transfers between devices, body(): mlp_all = lax.all_gather(mlp_in, 'tensor', axis=2, tiled=True)  81.3 us
    all_gather x1, waiting for transfers between devices, body(): lax.all_gather(grad_branch.astype(jnp.bfloat16), 'tensor', axis=2, tiled=...  81.3 us
  transfers between devices with their start and end apart: 14, of which 11 were waited for; matrix products, arithmetic and copies ran while one was open for 5% of the time, Pallas kernels for 0%

commit v1 on v0

--- a/solution.py
+++ b/solution.py
@@ -5,6 +5,19 @@
 from jax.sharding import PartitionSpec as P
 
 HD = 64
+
+
+def collect(value, axis, dim):
+    ways = lax.axis_size(axis)
+    up = [(d, (d + 1) % ways) for d in range(ways)]
+    down = [(d, (d - 1) % ways) for d in range(ways)]
+    earlier, later = ([value], [value])
+    for _ in range(ways // 2):
+        earlier.append(lax.ppermute(earlier[-1], axis, up))
+    for _ in range((ways - 1) // 2):
+        later.append(lax.ppermute(later[-1], axis, down))
+    line = jnp.concatenate([*earlier[::-1], *later[1:]], axis=dim)
+    return jnp.roll(line, (lax.axis_index(axis) - ways // 2) * value.shape[dim], axis=dim)
 
 
 def level_features(levels, context, frame_ids, breadth):
@@ -132,7 +145,7 @@
     hidden_one = block_input + gate_one * branch_one
     normed_two, inverse_two = normalize(hidden_one)
     mlp_in = (normed_two * (1.0 + scale_two) + shift_two).astype(jnp.bfloat16)
-    mlp_all = lax.all_gather(mlp_in, "tensor", axis=2, tiled=True)
+    mlp_all = collect(mlp_in, "tensor", 2)
     pre_act = jnp.einsum(
         "cfpd,de->cfpe", mlp_all, w_up, preferred_element_type=jnp.float32
     ) + b_up.astype(jnp.float32)

time: 1640 us -> 1640 us (level)
    all_gather x1 -> x0, waiting for transfers between devices: 81.3 us -> none  [body(): mlp_all = lax.all_gather(mlp_in, 'tensor', axis=2, tiled=True)]
    ppermute x0 -> x3, waiting for transfers between devices: none -> 66.1 us  [the longest x2 49.2 us: collect(): earlier.append(lax.ppermute(earlier[-1], axis, up))]
  transfers between devices with their start and end apart: 14 -> 16, of which waited for: 11 -> 13; matrix products, arithmetic and copies ran while one was open for 5% -> 5% of each run, Pallas kernels for 0% -> 0%
where the time goes in v1:
time: 1640 us; the launch traced here: 1630 us
  waiting for transfers between devices  726 us (44%)
  matrix products  534 us (33%)
  other arithmetic  245 us (15%)
  local copies, waits for them, and re-layouts  81.6 us (5%)
  blocking collectives  22.1 us (1%)
  between operations  16.4 us (1%)
    dot_general x8, matrix products, masked_scores(): jnp.einsum('bhd,khd->hbk', query_block, keys, preferred_element_type=jnp....  133 us
    convert_element_type x4, other arithmetic, backward_block(): grad_scores = (probability * (grad_prob - inner_sum)).astype(jnp.bfloat16)  111 us
    psum x1, waiting for transfers between devices, body(): lax.psum(grad_w_qkv.astype(jnp.bfloat16), ('dp', 'seq')).astype(jnp.float32)  107 us
    dot_general x4, matrix products, backward_block(): jnp.einsum('bhd,khd->hbk', grad_block, values, preferred_element_type=jnp...  104 us
    all_gather x1, waiting for transfers between devices, body(): attn_all = lax.all_gather(attn_in, 'tensor', axis=2, tiled=True)  83.5 us
    all_gather x1, waiting for transfers between devices, body(): grad_mlp_all = lax.all_gather(grad_mlp_low, 'tensor', axis=2, tiled=True)  81.4 us
    all_gather x1, waiting for transfers between devices, body(): lax.all_gather(grad_branch.astype(jnp.bfloat16), 'tensor', axis=2, tiled=...  81.3 us
    reduce_scatter x1, waiting for transfers between devices, body(): lax.psum_scatter(jnp.einsum('cfpe,ed->pcfd', portion, w_down, preferred_e...  77 us
  transfers between devices with their start and end apart: 16, of which 13 were waited for; matrix products, arithmetic and copies ran while one was open for 5% of the time, Pallas kernels for 0%

profile of v1, /device:TPU:0, one launch (start us, length us, event | category | flops | bytes accessed | tf_op | source)
XLA Modules:
  0.0 1632.6 jit_solution(8587661015781453267)
XLA Ops:
  12.0 6.5 fusion.60
  21.3 83.5 %all-gather.7.cloned.1.call-done = bf16[1,8,256,1024]{3,2,1,0:T(8,128)(2,1)} async-done(((bf16[1,8,64,1024]{3,2,1,0:T(8,128)(2,1)}), bf16[1,8,256,1024]{3,2,1,0:T(8,128)(2,1)}) %all-gather.7.cloned.1.call-update) | async-done | bytes 4194320 | tf_op jit(solution)/shard_map/all_gather | solution.py:82
  104.9 5.7 fusion.81
  147.6 198.1 %while.50 = (s32[]{:T(128)}, bf16[4,512,4,64]{1,3,2,0:T(8,128)(2,1)S(1)}, f32[4,4,512]{2,1,0:T(4,128)S(1)}, s32[4,512]{1,0:T(4,128)S(1)}, s32[]{:T(128)}, /*inde...) while((s32[]{:T(128)}, ...), condition=%wide.region_5.6_spmd.clone.clone, body=%wide.region_2.5_spmd.clone.clone.sunk | while | flops 2252539904 | bytes 122271888 | solution.py:129
  150.0 15.9 fusion.180
  165.9 15.0 fusion.181
  181.0 16.3 fusion.182
  199.5 15.9 fusion.180
  215.4 15.0 fusion.181
  230.4 16.3 fusion.182
  248.9 15.9 fusion.180
  264.9 15.0 fusion.181
  279.9 16.3 fusion.182
  298.4 15.9 fusion.180
  314.3 15.0 fusion.181
  329.4 16.3 fusion.182
  349.1 4.8 convert_bitcast_fusion.2
  354.0 76.8 %reduce-scatter.8.cloned.1.call-done = bf16[64,1,8,1024]{3,0,2,1:T(8,128)(2,1)} async-done(((bf16[256,1,8,1024]{3,0,2,1:T(8,128)(2,1)}), bf16[64,1,8,1024]{3,0,2,1:T(8,128)(2,1)}) %reduce-scatter.8.cloned.1.call-update) | async-done | bytes 1048592 | tf_op jit(solution)/shard_map/reduce_scatter | solution.py:136
  437.3 25.1 %collective-permute-done = bf16[1,8,64,1024]{3,2,1,0:T(8,128)(2,1)S(1)} collective-permute-done((bf16[1,8,64,1024]{3,2,1,0:T(8,128)(2,1)}, bf16[1,8,64,1024]{3,2,1,0:T(8,128)(2,1)S(1)}, u32[]{:S(2)}, u32[]{:S(2)}) %collective-permute-start) | collective-permute-done | bytes 1048608 | tf_op jit(solution)/shard_map/ppermute | solution.py:16
  466.2 24.1 %collective-permute-done.1 = bf16[1,8,64,1024]{3,2,1,0:T(8,128)(2,1)} collective-permute-done((bf16[1,8,64,1024]{3,2,1,0:T(8,128)(2,1)S(1)}, bf16[1,8,64,1024]{3,2,1,0:T(8,128)(2,1)}, u32[]{:S(2)}, u32[]{:S(2)}) %collective-permute-start.1) | collective-permute-done | bytes 1048608 | tf_op jit(solution)/shard_map/ppermute | solution.py:16
  492.2 16.8 %collective-permute-done.2 = bf16[1,8,64,1024]{3,2,1,0:T(8,128)(2,1)} collective-permute-done((bf16[1,8,64,1024]{3,2,1,0:T(8,128)(2,1)}, bf16[1,8,64,1024]{3,2,1,0:T(8,128)(2,1)}, u32[]{:S(2)}, u32[]{:S(2)}) %collective-permute-start.2) | collective-permute-done | bytes 1048608 | tf_op jit(solution)/shard_map/ppermute | solution.py:18
  517.0 4.6 fusion.75
  524.8 7.0 convert_bitcast_fusion.1
  532.5 77.0 %reduce-scatter.10.cloned.1.call-done = bf16[64,1,8,1024]{3,0,2,1:T(8,128)(2,1)} async-done(((bf16[256,1,8,1024]{3,0,2,1:T(8,128)(2,1)}), bf16[64,1,8,1024]{3,0,2,1:T(8,128)(2,1)}) %reduce-scatter.10.cloned.1.call-update) | async-done | bytes 1048592 | tf_op jit(solution)/shard_map/reduce_scatter | solution.py:154
  613.5 81.4 %all-gather.11.cloned.1.call-done = bf16[1,8,256,1024]{3,2,1,0:T(8,128)(2,1)} async-done(((bf16[1,8,64,1024]{3,2,1,0:T(8,128)(2,1)}), bf16[1,8,256,1024]{3,2,1,0:T(8,128)(2,1)}) %all-gather.11.cloned.1.call-update) | async-done | bytes 4194320 | tf_op jit(solution)/shard_map/all_gather | solution.py:168
  694.8 13.8 fusion.148
  710.7 6.2 convert_bitcast_fusion
  717.0 75.4 %reduce-scatter.12.cloned.1.call-done = bf16[64,1,8,1024]{3,0,2,1:T(8,128)(2,1)} async-done(((bf16[256,1,8,1024]{3,0,2,1:T(8,128)(2,1)}), bf16[64,1,8,1024]{3,0,2,1:T(8,128)(2,1)}) %reduce-scatter.12.cloned.1.call-update) | async-done | bytes 1048592 | tf_op jit(solution)/shard_map/reduce_scatter | solution.py:177
  802.5 81.3 %all-gather.13.cloned.1.call-done = bf16[1,8,256,1024]{3,2,1,0:T(8,128)(2,1)} async-done(((bf16[1,8,64,1024]{3,2,1,0:T(8,128)(2,1)}), bf16[1,8,256,1024]{3,2,1,0:T(8,128)(2,1)}) %all-gather.13.cloned.1.call-update) | async-done | bytes 4194320 | tf_op jit(solution)/shard_map/all_gather | solution.py:192
  891.6 436.1 %while.51 = (s32[]{:T(128)}, f32[4096,4,64]{0,2,1:T(8,128)}, f32[4096,4,64]{0,2,1:T(8,128)}, bf16[4,512,4,64]{1,3,2,0:T(8,128)(2,1)}, bf16[4,512,4,64]{1,3,2,0:T...) while((s32[]{:T(128)}, f32[4096,4,64]{0,2,1:T(8,128)}, ...), condition=%wide.region_15.16_spmd.clone.clone, body=%wide.region_13.15_spmd.clone.clone.sunk | while | flops 5504305152 | bytes 351639744 | solution.py:234
  894.0 17.3 %fusion.192 = f32[4,512,4096]{2,1,0:T(8,128)} fusion(bf16[4096,4,64]{0,2,1:T(8,128)(2,1)} %get-tuple-element.645, bf16[4,512,4,64]{1,3,2,0:T(8,128)(2,1)} %get-tuple-element.642, s32[]{:T(128)S(6)} %copy.138), kind=kOutput, calls=%fused_computation.48.clone.1 | convolution fusion | flops 1073741824 | bytes 35913732 | tf_op jit(solution)/shard_map/while/body/eval_jaxpr/while/body/eval_jaxpr/bhd,khd->hbk/dot_general | solution.py:106
  911.3 16.5 %fusion.194 = f32[4096,4,64]{0,2,1:T(8,128)} fusion(f32[4,512,4096]{2,1,0:T(8,128)} %fusion.192, f32[4,512]{1,0:T(4,128)S(1)} %dynamic-slice_bitcast_fusion.2, pred[512,4096]{1,0:T(8,128)(4,1)S(1)} %compare_or_fusion.5, f32[4096,4,64]{0,2,1:T(8,128)} %get-tuple-element.627, pred[]{:T(512)S(6)} %compare.10, ...), kind=kOutput, calls=%fused_computation.39.clone.1 | convolution fusion | flops 1109393408 | bytes 44310532 | tf_op jit(solution)/shard_map/while/body/eval_jaxpr/while/body/eval_jaxpr/hbk,bhd->khd/dot_general | solution.py:225
  927.8 26.0 %multiply_reduce_fusion.6 = (f32[4,512]{1,0:T(4,128)S(1)}, f32[4,512,4096]{2,1,0:T(8,128)}) fusion(f32[4,512,4096]{2,1,0:T(8,128)} %fusion.192, f32[4,512]{1,0:T(4,128)S(1)} %dynamic-slice_bitcast_fusion.2, pred[512,4096]{1,0:T(8,128)(4,1)S(1)} %compare_or_fusion.5, bf16[4096,4,64]{0,2,1:T(8,128)(2,1)} %get-tuple-element.648, ...), kind=kOutput, calls=%fused_computation.29.clone.1 | convolution fusion | flops 1115682816 | bytes 71581696 | tf_op jit(solution)/shard_map/while/body/eval_jaxpr/while/body/eval_jaxpr/bhd,khd->hbk/dot_general | solution.py:209
  953.8 27.6 %multiply_convert_fusion.10 = bf16[4,512,4096]{2,1,0:T(8,128)(2,1)} fusion(f32[4,512,4096]{2,1,0:T(8,128)} %get-tuple-element.583, f32[4,512,4096]{2,1,0:T(8,128)} %fusion.192, f32[4,512]{1,0:T(4,128)S(1)} %get-tuple-element.584, f32[4,512]{1,0:T(4,128)S(1)} %dynamic-slice_bitcast_fusion.2, pred[512,4096]{1,0:T(8,128)(4,1)S(1)} %compare_or_fusion.5), kind=kLoop, calls=%fused_computation.28.clone.1 | loop fusion | flops 50331648 | bytes 85999616 | tf_op jit(solution)/shard_map/while/body/eval_jaxpr/while/body/eval_jaxpr/convert_element_type | solution.py:213
  981.4 10.1 fusion.195
  992.7 6.1 fusion.193
  1001.0 17.3 %fusion.192 = f32[4,512,4096]{2,1,0:T(8,128)} fusion(bf16[4096,4,64]{0,2,1:T(8,128)(2,1)} %get-tuple-element.645, bf16[4,512,4,64]{1,3,2,0:T(8,128)(2,1)} %get-tuple-element.642, s32[]{:T(128)S(6)} %copy.138), kind=kOutput, calls=%fused_computation.48.clone.1 | convolution fusion | flops 1073741824 | bytes 35913732 | tf_op jit(solution)/shard_map/while/body/eval_jaxpr/while/body/eval_jaxpr/bhd,khd->hbk/dot_general | solution.py:106
  1018.3 17.7 %fusion.194 = f32[4096,4,64]{0,2,1:T(8,128)} fusion(f32[4,512,4096]{2,1,0:T(8,128)} %fusion.192, f32[4,512]{1,0:T(4,128)S(1)} %dynamic-slice_bitcast_fusion.2, pred[512,4096]{1,0:T(8,128)(4,1)S(1)} %compare_or_fusion.5, f32[4096,4,64]{0,2,1:T(8,128)} %get-tuple-element.627, pred[]{:T(512)S(6)} %compare.10, ...), kind=kOutput, calls=%fused_computation.39.clone.1 | convolution fusion | flops 1109393408 | bytes 44310532 | tf_op jit(solution)/shard_map/while/body/eval_jaxpr/while/body/eval_jaxpr/hbk,bhd->khd/dot_general | solution.py:225
  1036.0 26.0 %multiply_reduce_fusion.6 = (f32[4,512]{1,0:T(4,128)S(1)}, f32[4,512,4096]{2,1,0:T(8,128)}) fusion(f32[4,512,4096]{2,1,0:T(8,128)} %fusion.192, f32[4,512]{1,0:T(4,128)S(1)} %dynamic-slice_bitcast_fusion.2, pred[512,4096]{1,0:T(8,128)(4,1)S(1)} %compare_or_fusion.5, bf16[4096,4,64]{0,2,1:T(8,128)(2,1)} %get-tuple-element.648, ...), kind=kOutput, calls=%fused_computation.29.clone.1 | convolution fusion | flops 1115682816 | bytes 71581696 | tf_op jit(solution)/shard_map/while/body/eval_jaxpr/while/body/eval_jaxpr/bhd,khd->hbk/dot_general | solution.py:209
  1062.0 27.6 %multiply_convert_fusion.10 = bf16[4,512,4096]{2,1,0:T(8,128)(2,1)} fusion(f32[4,512,4096]{2,1,0:T(8,128)} %get-tuple-element.583, f32[4,512,4096]{2,1,0:T(8,128)} %fusion.192, f32[4,512]{1,0:T(4,128)S(1)} %get-tuple-element.584, f32[4,512]{1,0:T(4,128)S(1)} %dynamic-slice_bitcast_fusion.2, pred[512,4096]{1,0:T(8,128)(4,1)S(1)} %compare_or_fusion.5), kind=kLoop, calls=%fused_computation.28.clone.1 | loop fusion | flops 50331648 | bytes 85999616 | tf_op jit(solution)/shard_map/while/body/eval_jaxpr/while/body/eval_jaxpr/convert_element_type | solution.py:213
  1089.6 10.1 fusion.195
  1100.9 7.4 fusion.193
  1110.5 17.3 %fusion.192 = f32[4,512,4096]{2,1,0:T(8,128)} fusion(bf16[4096,4,64]{0,2,1:T(8,128)(2,1)} %get-tuple-element.645, bf16[4,512,4,64]{1,3,2,0:T(8,128)(2,1)} %get-tuple-element.642, s32[]{:T(128)S(6)} %copy.138), kind=kOutput, calls=%fused_computation.48.clone.1 | convolution fusion | flops 1073741824 | bytes 35913732 | tf_op jit(solution)/shard_map/while/body/eval_jaxpr/while/body/eval_jaxpr/bhd,khd->hbk/dot_general | solution.py:106
  1127.8 17.7 %fusion.194 = f32[4096,4,64]{0,2,1:T(8,128)} fusion(f32[4,512,4096]{2,1,0:T(8,128)} %fusion.192, f32[4,512]{1,0:T(4,128)S(1)} %dynamic-slice_bitcast_fusion.2, pred[512,4096]{1,0:T(8,128)(4,1)S(1)} %compare_or_fusion.5, f32[4096,4,64]{0,2,1:T(8,128)} %get-tuple-element.627, pred[]{:T(512)S(6)} %compare.10, ...), kind=kOutput, calls=%fused_computation.39.clone.1 | convolution fusion | flops 1109393408 | bytes 44310532 | tf_op jit(solution)/shard_map/while/body/eval_jaxpr/while/body/eval_jaxpr/hbk,bhd->khd/dot_general | solution.py:225
  1145.5 26.0 %multiply_reduce_fusion.6 = (f32[4,512]{1,0:T(4,128)S(1)}, f32[4,512,4096]{2,1,0:T(8,128)}) fusion(f32[4,512,4096]{2,1,0:T(8,128)} %fusion.192, f32[4,512]{1,0:T(4,128)S(1)} %dynamic-slice_bitcast_fusion.2, pred[512,4096]{1,0:T(8,128)(4,1)S(1)} %compare_or_fusion.5, bf16[4096,4,64]{0,2,1:T(8,128)(2,1)} %get-tuple-element.648, ...), kind=kOutput, calls=%fused_computation.29.clone.1 | convolution fusion | flops 1115682816 | bytes 71581696 | tf_op jit(solution)/shard_map/while/body/eval_jaxpr/while/body/eval_jaxpr/bhd,khd->hbk/dot_general | solution.py:209
  1171.5 27.6 %multiply_convert_fusion.10 = bf16[4,512,4096]{2,1,0:T(8,128)(2,1)} fusion(f32[4,512,4096]{2,1,0:T(8,128)} %get-tuple-element.583, f32[4,512,4096]{2,1,0:T(8,128)} %fusion.192, f32[4,512]{1,0:T(4,128)S(1)} %get-tuple-element.584, f32[4,512]{1,0:T(4,128)S(1)} %dynamic-slice_bitcast_fusion.2, pred[512,4096]{1,0:T(8,128)(4,1)S(1)} %compare_or_fusion.5), kind=kLoop, calls=%fused_computation.28.clone.1 | loop fusion | flops 50331648 | bytes 85999616 | tf_op jit(solution)/shard_map/while/body/eval_jaxpr/while/body/eval_jaxpr/convert_element_type | solution.py:213
  1199.2 10.1 fusion.195
  1210.4 7.4 fusion.193
  1220.0 17.3 %fusion.192 = f32[4,512,4096]{2,1,0:T(8,128)} fusion(bf16[4096,4,64]{0,2,1:T(8,128)(2,1)} %get-tuple-element.645, bf16[4,512,4,64]{1,3,2,0:T(8,128)(2,1)} %get-tuple-element.642, s32[]{:T(128)S(6)} %copy.138), kind=kOutput, calls=%fused_computation.48.clone.1 | convolution fusion | flops 1073741824 | bytes 35913732 | tf_op jit(solution)/shard_map/while/body/eval_jaxpr/while/body/eval_jaxpr/bhd,khd->hbk/dot_general | solution.py:106
  1237.3 17.7 %fusion.194 = f32[4096,4,64]{0,2,1:T(8,128)} fusion(f32[4,512,4096]{2,1,0:T(8,128)} %fusion.192, f32[4,512]{1,0:T(4,128)S(1)} %dynamic-slice_bitcast_fusion.2, pred[512,4096]{1,0:T(8,128)(4,1)S(1)} %compare_or_fusion.5, f32[4096,4,64]{0,2,1:T(8,128)} %get-tuple-element.627, pred[]{:T(512)S(6)} %compare.10, ...), kind=kOutput, calls=%fused_computation.39.clone.1 | convolution fusion | flops 1109393408 | bytes 44310532 | tf_op jit(solution)/shard_map/while/body/eval_jaxpr/while/body/eval_jaxpr/hbk,bhd->khd/dot_general | solution.py:225
  1255.0 26.0 %multiply_reduce_fusion.6 = (f32[4,512]{1,0:T(4,128)S(1)}, f32[4,512,4096]{2,1,0:T(8,128)}) fusion(f32[4,512,4096]{2,1,0:T(8,128)} %fusion.192, f32[4,512]{1,0:T(4,128)S(1)} %dynamic-slice_bitcast_fusion.2, pred[512,4096]{1,0:T(8,128)(4,1)S(1)} %compare_or_fusion.5, bf16[4096,4,64]{0,2,1:T(8,128)(2,1)} %get-tuple-element.648, ...), kind=kOutput, calls=%fused_computation.29.clone.1 | convolution fusion | flops 1115682816 | bytes 71581696 | tf_op jit(solution)/shard_map/while/body/eval_jaxpr/while/body/eval_jaxpr/bhd,khd->hbk/dot_general | solution.py:209
  1281.0 27.6 %multiply_convert_fusion.10 = bf16[4,512,4096]{2,1,0:T(8,128)(2,1)} fusion(f32[4,512,4096]{2,1,0:T(8,128)} %get-tuple-element.583, f32[4,512,4096]{2,1,0:T(8,128)} %fusion.192, f32[4,512]{1,0:T(4,128)S(1)} %get-tuple-element.584, f32[4,512]{1,0:T(4,128)S(1)} %dynamic-slice_bitcast_fusion.2, pred[512,4096]{1,0:T(8,128)(4,1)S(1)} %compare_or_fusion.5), kind=kLoop, calls=%fused_computation.28.clone.1 | loop fusion | flops 50331648 | bytes 85999616 | tf_op jit(solution)/shard_map/while/body/eval_jaxpr/while/body/eval_jaxpr/convert_element_type | solution.py:213
  1308.7 10.1 fusion.195
  1319.9 7.4 fusion.193
  1348.2 10.3 reduce-scatter.16.cloned.1.call-done
  1358.6 7.5 fusion.61
  1366.3 9.5 bitcast_convert_fusion.2
  1375.9 11.0 bitcast_convert_fusion.1
  1389.3 55.0 %reduce-scatter.18.cloned.1.call-done = bf16[64,1,8,1024]{3,0,2,1:T(8,128)(2,1)} async-done(((bf16[256,1,8,1024]{3,0,2,1:T(8,128)(2,1)}), bf16[64,1,8,1024]{3,0,2,1:T(8,128)(2,1)}) %reduce-scatter.18.cloned.1.call-update) | async-done | bytes 1048592 | tf_op jit(solution)/shard_map/reduce_scatter | solution.py:272
  1449.1 7.5 bitcast_convert_fusion.3
  1456.5 12.5 reduce-scatter.20.cloned.1.call-done
  1474.4 8.9 all-reduce.4
  1488.1 13.2 all-reduce.2
  1504.3 106.9 %all-reduce.7.cloned.1.call-done = (bf16[1024,3,256]{2,0,1:T(8,128)(2,1)}, bf16[256,1024]{1,0:T(8,128)(2,1)}, bf16[1024,1024]{1,0:T(8,128)(2,1)}, bf16[1024,1024]{1,0:T(8,128)(2,1)}, bf16[1024,1536]{1,0:T(8,128)(2,1)}) async-done(((bf16[1024,3,256]{2,0,1:T(8,128)(2,1)}, bf16[256,1024]{1,0:T(8,128)(2,1)}, bf16[1024,1024]{1,0:T(8,128)(2,1)}, bf16[1024,1024]{1,0:T(8,128)(2,1)}, bf16[1024,1536]{1,0:T(8,128)(2,1)}), ...) | async-done | bytes 9437200 | tf_op jit(solution)/shard_map/psum | solution.py:322
  (301 shorter events, 171.5 us)
Async XLA Ops:
  7.2 517.7 %copy-start = (bf16[1024,1024]{1,0:T(8,128)(2,1)S(1)}, bf16[1024,1024]{1,0:T(8,128)(2,1)}, u32[]{:S(2)}) copy-start(bf16[1024,1024]{1,0:T(8,128)(2,1)} %param.25) | copy-start | bytes 6291460
  7.2 4.6 copy-start.43
  7.2 4.6 copy-start.53
  7.2 97.7 %all-gather.7.cloned.1.call-start = ((), (), s32[]{:S(2)}) async-start(), calls=%async_computation.7 | async-start | bytes 5242880 | tf_op jit(solution)/shard_map/all_gather | solution.py:82
  9.8 9.3 copy-start.35
  11.8 7.4 copy-start.38
  12.0 6.5 copy-start.29
  12.0 6.5 copy-start.31
  12.0 7.7 copy-start.7
  21.3 108.8 %all-gather.9.cloned.1.call-start = ((), (), s32[]{:S(2)}) async-start(), calls=%async_computation.8 | async-start | bytes 3145728 | tf_op jit(solution)/shard_map/all_gather | solution.py:90
  114.4 24.4 %all-gather.15.cloned.1.call-start = ((), (), s32[]{:S(2)}) async-start(), calls=%async_computation.18 | async-start | bytes 3145728 | tf_op jit(solution)/shard_map/all_gather | solution.py:89
  117.2 313.5 %reduce-scatter.8.cloned.1.call-start = ((), (), s32[]{:S(2)}) async-start(), calls=%async_computation.9 | async-start | bytes 5242880 | tf_op jit(solution)/shard_map/reduce_scatter | solution.py:136
  150.0 15.9 copy-start.3
  199.5 15.9 copy-start.3
  248.9 15.9 copy-start.3
  298.4 15.9 copy-start.3
  349.0 4.8 copy-start.16
  349.0 4.9 copy-start.49
  349.0 81.7 %copy-start.25 = (f32[8,1024]{1,0:T(8,128)S(1)}, f32[8,1024]{1,0:T(8,128)}, u32[]{:S(2)}) copy-start(f32[8,1024]{1,0:T(8,128)} %get-tuple-element.454) | copy-start | bytes 98308
  353.9 80.5 %copy-start.22 = (f32[8,1024]{1,0:T(8,128)S(1)}, f32[8,1024]{1,0:T(8,128)}, u32[]{:S(2)}) copy-start(f32[8,1024]{1,0:T(8,128)} %get-tuple-element.451) | copy-start | bytes 98308
  353.9 80.5 %copy-start.26 = (f32[8,1024]{1,0:T(8,128)S(1)}, f32[8,1024]{1,0:T(8,128)}, u32[]{:S(2)}) copy-start(f32[8,1024]{1,0:T(8,128)} %get-tuple-element.450) | copy-start | bytes 98308
  353.9 255.6 %reduce-scatter.10.cloned.1.call-start = ((), (), s32[]{:S(2)}) async-start(), calls=%async_computation.10 | async-start | bytes 5242880 | tf_op jit(solution)/shard_map/reduce_scatter | solution.py:154
  430.7 35.5 %copy-start.50 = (bf16[1024]{0:T(1024)(128)(2,1)S(1)}, bf16[1024]{0:T(1024)(128)(2,1)}, u32[]{:S(2)}) copy-start(bf16[1024]{0:T(1024)(128)(2,1)} %param.24) | copy-start | bytes 6148
  435.8 26.6 %collective-permute-start = (bf16[1,8,64,1024]{3,2,1,0:T(8,128)(2,1)}, bf16[1,8,64,1024]{3,2,1,0:T(8,128)(2,1)S(1)}, u32[]{:S(2)}, u32[]{:S(2)}) collective-permute-start(bf16[1,8,64,1024]{3,2,1,0:T(8,128)(2,1)} %add_convert_fusion), channel_id=1, source_target_pairs={{0,1},{1,2},{2,3},{3,0},{4,5},{5,6},{6,7},{7,4},{8,9},{9,10},{10,1... | collective-permute-start | bytes 3145736 | tf_op jit(solution)/shard_map/ppermute | solution.py:16
  462.4 27.9 %collective-permute-start.1 = (bf16[1,8,64,1024]{3,2,1,0:T(8,128)(2,1)S(1)}, bf16[1,8,64,1024]{3,2,1,0:T(8,128)(2,1)}, u32[]{:S(2)}, u32[]{:S(2)}) collective-permute-start(bf16[1,8,64,1024]{3,2,1,0:T(8,128)(2,1)S(1)} %collective-permute-done), channel_id=1, source_target_pairs={{0,1},{1,2},{2,3},{3,0},{4,5},{5,6},{6,7},{7,4},{8,9},{9,10},{10,1... | collective-permute-start | bytes 3145736 | tf_op jit(solution)/shard_map/ppermute | solution.py:16
  462.4 46.7 %collective-permute-start.2 = (bf16[1,8,64,1024]{3,2,1,0:T(8,128)(2,1)}, bf16[1,8,64,1024]{3,2,1,0:T(8,128)(2,1)}, u32[]{:S(2)}, u32[]{:S(2)}) collective-permute-start(bf16[1,8,64,1024]{3,2,1,0:T(8,128)(2,1)} %add_convert_fusion), channel_id=1, source_target_pairs={{0,3},{1,0},{2,1},{3,2},{4,7},{5,4},{6,5},{7,6},{8,11},{9,8},{10,9... | collective-permute-start | bytes 3145736 | tf_op jit(solution)/shard_map/ppermute | solution.py:18
  466.2 228.6 %copy-start.47 = (f32[1024]{0:T(1024)}, f32[1024]{0:T(1024)S(1)}, u32[]{:S(2)}) copy-start(f32[1024]{0:T(1024)S(1)} %convert_element_type.268) | copy-start | bytes 12292
  466.2 25.5 %copy-start.5 = (f32[1,8,64,1024]{3,2,1,0:T(8,128)S(1)}, f32[1,8,64,1024]{3,2,1,0:T(8,128)}, u32[]{:S(2)}) copy-start(f32[1,8,64,1024]{3,2,1,0:T(8,128)} %copy-done.4) | copy-start | bytes 6291460
  511.8 5.3 copy-start.56
  513.7 3.3 copy-start.34
  531.8 77.7 %copy-start.28 = (f32[8,1024]{1,0:T(8,128)S(1)}, f32[8,1024]{1,0:T(8,128)}, u32[]{:S(2)}) copy-start(f32[8,1024]{1,0:T(8,128)} %get-tuple-element.449) | copy-start | bytes 98308
  531.8 163.0 %all-gather.11.cloned.1.call-start = ((), (), s32[]{:S(2)}) async-start(), calls=%async_computation.11 | async-start | bytes 5242880 | tf_op jit(solution)/shard_map/all_gather | solution.py:168
  613.4 179.0 %reduce-scatter.12.cloned.1.call-start = ((), (), s32[]{:S(2)}) async-start(), calls=%async_computation.12 | async-start | bytes 5242880 | tf_op jit(solution)/shard_map/reduce_scatter | solution.py:177
  694.8 15.9 copy-start.57
  716.9 75.5 %copy-start.6 = (f32[1,8,64,1024]{3,2,1,0:T(8,128)S(1)}, f32[1,8,64,1024]{3,2,1,0:T(8,128)}, u32[]{:S(2)}) copy-start(f32[1,8,64,1024]{3,2,1,0:T(8,128)} %copy-done.4) | copy-start | bytes 6291460
  716.9 78.4 %copy-start.18 = (bf16[64,1,8,1024]{3,0,2,1:T(8,128)(2,1)S(1)}, bf16[64,1,8,1024]{3,0,2,1:T(8,128)(2,1)}, u32[]{:S(2)}) copy-start(bf16[64,1,8,1024]{3,0,2,1:T(8,128)(2,1)} %reduce-scatter.8.cloned.1.call-done) | copy-start | bytes 3145732
  716.9 166.9 %all-gather.13.cloned.1.call-start = ((), (), s32[]{:S(2)}) async-start(), calls=%async_computation.13 | async-start | bytes 5242880 | tf_op jit(solution)/shard_map/all_gather | solution.py:192
  799.8 84.0 %copy-start.27 = (bf16[256,1024]{1,0:T(8,128)(2,1)S(1)}, bf16[256,1024]{1,0:T(8,128)(2,1)}, u32[]{:S(2)}) copy-start(bf16[256,1024]{1,0:T(8,128)(2,1)} %param.21) | copy-start | bytes 1572868
  802.5 545.8 %reduce-scatter.14.cloned.1.call-start = ((), (), s32[]{:S(2)}) async-start(), calls=%async_computation.14 | async-start | bytes 3145728 | tf_op jit(solution)/shard_map/reduce_scatter | solution.py:246
  981.4 11.2 copy-start.2
  1089.6 11.2 copy-start.2
  1199.2 11.2 copy-start.2
  1308.7 11.2 copy-start.2
  1336.4 22.1 %reduce-scatter.16.cloned.1.call-start = ((), (), s32[]{:S(2)}) async-start(), calls=%async_computation.15 | async-start | bytes 3145728 | tf_op jit(solution)/shard_map/reduce_scatter | solution.py:252
  1340.9 4.5 copy-start.15
  1345.4 99.0 %reduce-scatter.18.cloned.1.call-start = ((), (), s32[]{:S(2)}) async-start(), calls=%async_computation.16 | async-start | bytes 5242880 | tf_op jit(solution)/shard_map/reduce_scatter | solution.py:272
  1366.1 9.8 copy-start.48
  1366.1 102.9 %reduce-scatter.20.cloned.1.call-start = ((), (), s32[]{:S(2)}) async-start(), calls=%async_computation.17 | async-start | bytes 122880 | tf_op jit(solution)/shard_map/reduce_scatter | solution.py:297
  1366.3 9.5 copy-start.54
  1375.9 11.1 copy-start.12
  1375.9 11.3 copy-start.17
  1375.9 11.3 copy-start.55
  1387.2 58.6 %copy-start.8 = (f32[1,8,64,1024]{3,2,1,0:T(8,128)S(1)}, f32[1,8,64,1024]{3,2,1,0:T(8,128)}, u32[]{:S(2)}) copy-start(f32[1,8,64,1024]{3,2,1,0:T(8,128)} %param.18) | copy-start | bytes 6291460
  1387.2 58.6 %copy-start.24 = (f32[8,1024]{1,0:T(8,128)S(1)}, f32[8,1024]{1,0:T(8,128)}, u32[]{:S(2)}) copy-start(f32[8,1024]{1,0:T(8,128)} %copy-done.23) | copy-start | bytes 98308
  1387.2 58.6 %copy-start.36 = (f32[8,64]{1,0:T(8,128)S(1)}, f32[8,64]{1,0:T(8,128)}, u32[]{:S(2)}) copy-start(f32[8,64]{1,0:T(8,128)} %copy-done.35) | copy-start | bytes 6148
  1387.2 58.6 %copy-start.39 = (f32[8,64]{1,0:T(8,128)S(1)}, f32[8,64]{1,0:T(8,128)}, u32[]{:S(2)}) copy-start(f32[8,64]{1,0:T(8,128)} %copy-done.38) | copy-start | bytes 6148
  1389.3 59.0 %copy-start.42 = (bf16[8,1024]{1,0:T(8,128)(2,1)S(1)}, bf16[8,1024]{1,0:T(8,128)(2,1)}, u32[]{:S(2)}) copy-start(bf16[8,1024]{1,0:T(8,128)(2,1)} %get-tuple-element.386) | copy-start | bytes 49156
  1389.3 59.0 %copy-start.41 = (bf16[8,1024]{1,0:T(8,128)(2,1)S(1)}, bf16[8,1024]{1,0:T(8,128)(2,1)}, u32[]{:S(2)}) copy-start(bf16[8,1024]{1,0:T(8,128)(2,1)} %get-tuple-element.380) | copy-start | bytes 49156
  1389.3 59.0 %copy-start.40 = (bf16[8,1024]{1,0:T(8,128)(2,1)S(1)}, bf16[8,1024]{1,0:T(8,128)(2,1)}, u32[]{:S(2)}) copy-start(bf16[8,1024]{1,0:T(8,128)(2,1)} %get-tuple-element.384) | copy-start | bytes 49156
  1449.0 20.1 %copy-start.30 = (f32[8,512]{1,0:T(8,128)S(1)}, f32[8,512]{1,0:T(8,128)}, u32[]{:S(2)}) copy-start(f32[8,512]{1,0:T(8,128)} %copy-done.29) | copy-start | bytes 49156
  1449.0 20.0 %copy-start.32 = (f32[8,512]{1,0:T(8,128)S(1)}, f32[8,512]{1,0:T(8,128)}, u32[]{:S(2)}) copy-start(f32[8,512]{1,0:T(8,128)} %copy-done.31) | copy-start | bytes 49156
  1449.0 162.1 %all-reduce.7.cloned.1.call-start = ((), (), s32[]{:S(2)}) async-start(), calls=%async_computation.19 | async-start | bytes 18874368 | tf_op jit(solution)/shard_map/psum | solution.py:322
  1611.1 5.6 copy-start.21
  1621.7 4.1 copy-start.1
  (19 other events, 37.8 us)
Sparse Core Ops, SparseCore 0:
  21.4 83.4 all-gather.6
  114.6 9.0 all-gather.8
  125.8 11.7 all-gather.14
  354.0 76.7 reduce-scatter.7
  532.0 77.4 reduce-scatter.9
  613.5 81.2 all-gather.10
  717.1 75.2 reduce-scatter.11
  802.6 81.2 all-gather.12
  1336.6 8.2 reduce-scatter.13
  1347.5 11.0 reduce-scatter.15
  1366.2 78.0 reduce-scatter.17
  1449.1 19.8 reduce-scatter.19
  1474.5 136.5 all-reduce.6
